TPU v7x, 32 devices: a whole 2x2x4 slice. The times are simulated.
32 devices in a mesh: grp: 2 (over y), ctx: 4 (over z), chan: 4 (over x, core).
Axes of the slice: x: 2, y: 2, z: 4, core: 2. Of those that a mesh axis runs over, the one named last changes fastest.
Arguments:
- grad_out: bfloat16 [1024, 4096], P(('grp', 'ctx'), 'chan'), parts along dimension 0, may hold values from -6 to 6
- gate_act: bfloat16 [1024, 4096], P(('grp', 'ctx'), 'chan'), parts along dimension 0, may hold values from -6 to 6
- conv_input: bfloat16 [1024, 4096], P(('grp', 'ctx'), 'chan'), parts along dimension 0, may hold values from -0.26367188 to 0.26367188
- filter_taps: bfloat16 [512, 4096], P('ctx', 'chan'), may hold values from -0.26367188 to 0.26367188
- skip_gain: float32 [4096], P('chan'), may hold values from -4 to 4
Outputs:
- grad_input: bfloat16 [1024, 4096], P(('grp', 'ctx'), 'chan'), parts along dimension 0
- grad_filter: float32 [1024, 4096], P(('grp', 'ctx'), 'chan'), parts along dimension 0
There are 2 independent parts, one for each index of `grp`. A program takes and returns all parts, laid end to end along the dimension named above; an argument that names none is the same for every part. Nothing has to cross between parts.
All inputs are finite; a program needn't handle non-finite values.
Results may differ from a plain program's by a relative error of at most 0.014.
Values may be sent and summed in bfloat16 or wider, within the bound.
No kernel may reach another device: no remote copies, remote signals or barrier semaphores. Data moves between devices by JAX's collectives and lax.ppermute only.
A program may use at most 64 MiB of HBM per device.

v0:
```python
import jax
import jax.numpy as jnp
from jax import lax
from jax.sharding import PartitionSpec as P


def split_parts(values):
    high_part = values.astype(jnp.bfloat16)
    low_part = (values - high_part.astype(jnp.float32)).astype(jnp.bfloat16)
    return (high_part, low_part)


def phase_tables(row_count, col_count, shift, period):
    row_index = jnp.arange(row_count, dtype=jnp.int32)[:, None] + shift
    col_index = jnp.arange(col_count, dtype=jnp.int32)[None, :]
    angles = (row_index * col_index % period).astype(jnp.float32) * (2.0 * jnp.pi / period)
    return (split_parts(jnp.cos(angles)), split_parts(jnp.sin(angles)))


def table_times(table, signal):
    high_part, low_part = table
    return jnp.dot(high_part, signal, preferred_element_type=jnp.float32) + jnp.dot(
        low_part, signal, preferred_element_type=jnp.float32
    )


def table_times_float(table, values):
    high_part, low_part = table
    value_high, value_low = split_parts(values)
    total = jnp.dot(high_part, value_high, preferred_element_type=jnp.float32)
    total = total + jnp.dot(high_part, value_low, preferred_element_type=jnp.float32)
    return total + jnp.dot(low_part, value_high, preferred_element_type=jnp.float32)


def forward_spectra(tables, signal):
    cos_part, sin_part = tables
    return (table_times(cos_part, signal), -table_times(sin_part, signal))


def inverse_spectra(tables, spectra, period):
    cos_part, sin_part = tables
    return (
        table_times_float(cos_part, spectra[0]) - table_times_float(sin_part, spectra[1])
    ) / period


def batched_times(table, blocks):
    high_part, low_part = table
    return jnp.einsum(
        "pr,nrc->npc", high_part, blocks, preferred_element_type=jnp.float32
    ) + jnp.einsum("pr,nrc->npc", low_part, blocks, preferred_element_type=jnp.float32)


def times_conj(first_spec, second_spec):
    return (
        first_spec[0] * second_spec[0] + first_spec[1] * second_spec[1],
        first_spec[1] * second_spec[0] - first_spec[0] * second_spec[1],
    )


def shards(grad_out, gate_act, conv_input, filter_taps, skip_gain):
    span_len = grad_out.shape[0]
    channels = grad_out.shape[1]
    period = 2 * span_len
    cycle_size = lax.axis_size("ctx")
    own_index = lax.axis_index("ctx")
    grad_y = (grad_out.astype(jnp.float32) * gate_act.astype(jnp.float32)).astype(jnp.bfloat16)
    short_fwd = phase_tables(period, span_len, 0, period)
    full_fwd = phase_tables(period, period, 0, period)
    short_inv = phase_tables(span_len, period, span_len, period)
    full_inv = phase_tables(period, period, span_len, period)
    taps = lax.all_gather(filter_taps, "ctx", axis=0, tiled=True)
    taps_padded = jnp.concatenate([jnp.zeros((span_len, channels), jnp.bfloat16), taps], axis=0)
    windows = jnp.concatenate(
        [
            taps_padded[:-span_len].reshape(cycle_size, span_len, channels),
            taps_padded[span_len:].reshape(cycle_size, span_len, channels),
        ],
        axis=1,
    )
    window_real = batched_times(full_fwd[0], windows)
    window_imag = -batched_times(full_fwd[1], windows)
    own_input_spec = forward_spectra(short_fwd, conv_input)
    zero_spec = jnp.zeros((period, channels), jnp.float32)
    lag_sums = jnp.zeros((taps_padded.shape[0], channels), jnp.float32)

    def add_pair(lag_totals, grad_spec, input_spec, distance):
        window_spec = (
            lax.dynamic_index_in_dim(window_real, distance, 0, keepdims=False),
            lax.dynamic_index_in_dim(window_imag, distance, 0, keepdims=False),
        )
        product = times_conj(grad_spec, window_spec)
        start_row = distance * span_len
        lag_window = inverse_spectra(full_inv, times_conj(grad_spec, input_spec), period)
        current = lax.dynamic_slice_in_dim(lag_totals, start_row, period, 0)
        lag_totals = lax.dynamic_update_slice_in_dim(lag_totals, current + lag_window, start_row, 0)
        return (product, lag_totals)

    spans = lax.all_gather(grad_y[None], "ctx", axis=0, tiled=True)

    def span_step(offset, current):
        distance = offset - own_index

        def run_pair(values_now):
            arrived = lax.dynamic_index_in_dim(spans, offset, 0, keepdims=False)
            product, new_sums = add_pair(
                values_now[2], forward_spectra(short_fwd, arrived), own_input_spec, distance
            )
            return (values_now[0] + product[0], values_now[1] + product[1], new_sums)

        return lax.cond(distance >= 0, run_pair, lambda values_now: values_now, current)

    home_real, home_imag, lag_sums = lax.fori_loop(
        0, spans.shape[0], span_step, (zero_spec, zero_spec, lag_sums)
    )
    conv_part = inverse_spectra(short_inv, (home_real, home_imag), period)
    grad_input = (conv_part + skip_gain[None, :] * grad_y.astype(jnp.float32)).astype(jnp.bfloat16)
    grad_filter = lax.psum_scatter(
        lag_sums[span_len:].astype(jnp.bfloat16), "ctx", scatter_dimension=0, tiled=True
    ).astype(jnp.float32)
    return (grad_input, grad_filter)


def solution(mesh):
    return jax.shard_map(
        shards,
        mesh=mesh,
        in_specs=(
            P(("grp", "ctx"), "chan"),
            P(("grp", "ctx"), "chan"),
            P(("grp", "ctx"), "chan"),
            P("ctx", "chan"),
            P("chan"),
        ),
        out_specs=(P(("grp", "ctx"), "chan"), P(("grp", "ctx"), "chan")),
        check_vma=False,
    )
```

profile of v0, /device:TPU:0, one launch (start us, length us, event | category | flops | bytes accessed | tf_op | source)
XLA Modules:
  0.0 181.5 jit_solution(1788791915903343266)
XLA Ops:
  8.0 1.8 multiply_convert_fusion
  10.6 0.7 fusion.117
  11.3 0.7 convolution_add_fusion.7
  12.0 0.7 fusion.70
  12.7 1.4 copy.12
  14.1 1.3 copy.13
  15.4 24.8 %all-gather.4.cloned.1.call-done = bf16[512,1024]{1,0:T(8,128)(2,1)} async-done(((bf16[128,1024]{1,0:T(8,128)(2,1)}), bf16[512,1024]{1,0:T(8,128)(2,1)}) %all-gather.4.cloned.1.call-update) | async-done | bytes 1048592 | tf_op jit(solution)/shard_map/all_gather | solution.py:72
  40.2 1.3 pad_slice_fusion
  41.6 0.8 copy.10
  43.1 1.6 fusion.93
  44.8 1.7 fusion.91
  46.4 3.6 %add_bitcast_fusion = f32[4,256,1024]{1,2,0:T(8,128)} fusion(f32[4,1024,256]{2,1,0:T(8,128)S(1)} %fusion.93, bf16[4,128,1024]{1,2,0:T(8,128)(2,1)S(1)} %copy.11, bf16[4,128,1024]{1,2,0:T(8,128)(2,1)S(1)} %copy.10), kind=kOutput, calls=%fused_computation.87 | convolution fusion | flops 543293440 | bytes 10485760 | tf_op jit(solution)/shard_map/pr,nrc->npc/dot_general | solution.py:51
  50.0 3.7 %negate_bitcast_fusion = f32[4,256,1024]{1,2,0:T(8,128)} fusion(f32[4,1024,256]{2,1,0:T(8,128)S(1)} %fusion.91, bf16[4,128,1024]{1,2,0:T(8,128)(2,1)S(1)} %copy.11, bf16[4,128,1024]{1,2,0:T(8,128)(2,1)S(1)} %copy.10), kind=kOutput, calls=%fused_computation.86 | convolution fusion | flops 544342016 | bytes 10485760 | tf_op jit(solution)/shard_map/pr,nrc->npc/dot_general | solution.py:51
  53.7 16.3 %all-gather.6.cloned.1.call-done = bf16[512,1024]{1,0:T(8,128)(2,1)} async-done(((bf16[128,1024]{1,0:T(8,128)(2,1)}), bf16[512,1024]{1,0:T(8,128)(2,1)}) %all-gather.6.cloned.1.call-update) | async-done | bytes 1048592 | tf_op jit(solution)/shard_map/all_gather | solution.py:99
  70.0 1.7 broadcast_in_dim.7
  71.8 1.0 broadcast_in_dim.6
  72.8 1.1 broadcast_in_dim.6.clone
  73.9 70.8 %while.20 = (s32[]{:T(128)}, f32[256,1024]{0,1:T(8,128)}, f32[256,1024]{0,1:T(8,128)}, f32[640,1024]{0,1:T(8,128)}, s32[]{:T(128)}, /*index=5*/bf16[4,128,1024]{...) while((s32[]{:T(128)}, f32[256,1024]{0,1:T(8,128)}, ...), condition=%wide.region_3.4_spmd.clone.clone.clone, body=%wide.region_0.3_spmd.clone.clone.clone.sunk | while | flops 1085865984 | bytes 40109640 | solution.py:113
  73.9 1.9 %subtract_convert_fusion.25 = (bf16[256,256]{1,0:T(8,128)(2,1)}, bf16[256,256]{1,0:T(8,128)(2,1)}, bf16[256,256]{1,0:T(8,128)(2,1)S(1)}, bf16[256,256]{1,0:T(8,128)(2,1)}) fusion(s32[256]{0:T(256)S(1)} %get-tuple-element.688), kind=kLoop, calls=%fused_computation.62.clone.1 | loop fusion | flops 1441792 | bytes 525312 | tf_op jit(solution)/shard_map/convert_element_type | solution.py:9
  75.8 1.2 fusion.214
  77.0 1.2 subtract_convert_fusion.24
  78.1 13.5 %conditional.5 = ((f32[256,1024]{0,1:T(8,128)}, f32[256,1024]{0,1:T(8,128)}, f32[640,1024]{0,1:T(8,128)})) conditional(s32[]{:T(128)} %convert_element_type.670, (f32[256,1024]{0,1:T(8,128)}, f32[256,1024]{0,1:T(8,128)}, f32[640,1024]{0,1:T(8,128)}) %tuple.73, (s32[]{:T(128)}, bf16[4,128,1024]{2,1,0:T(8,128)(2,1)}, bf16[256,128]{1,0:T(8,128)(2,1)}, ...), branch_computations={%region_1.1_spmd, %region_2.2_spmd} | conditional | flops 1083179008 | bytes 39321852 | solution.py:111
  78.1 1.3 fusion.29
  79.4 1.3 fusion.22
  80.7 1.3 fusion.32
  82.0 5.0 %multiply_subtract_fusion = (f32[256,1024]{0,1:T(8,128)S(1)}, f32[256,1024]{0,1:T(8,128)S(1)}, f32[256,1024]{0,1:T(8,128)}, f32[256,1024]{0,1:T(8,128)}) fusion(f32[256,1024]{0,1:T(8,128)} %get-tuple-element.336, f32[256,1024]{0,1:T(8,128)S(1)} %fusion.22, f32[256,1024]{0,1:T(8,128)} %get-tuple-element.335, f32[256,1024]{0,1:T(8,128)} %get-tuple-element.323, ...), kind=kOutput, calls=%fused_computation.31 | convolution fusion | flops 71041024 | bytes 12910600 | tf_op jit(solution)/shard_map/while/body/eval_jaxpr/cond/branch_1_fun/dot_general | solution.py:22
  88.9 2.7 %fusion.20 = f32[640,1024]{0,1:T(8,128)} fusion(f32[640,1024]{0,1:T(8,128)} %get-tuple-element.334, s32[]{:T(128)S(6)} %select_n.24, f32[1024,256]{1,0:T(8,128)S(1)} %convolution_add_fusion.2, f32[1024,256]{1,0:T(8,128)S(1)} %convolution_add_fusion.1, bf16[256,256]{1,0:T(8,128)(2,1)S(1)} %copy-done.2, f32[256,1024]{0,1:T(8,128)S(1)} %get-tuple-element.545), kind=kOutput, calls=%fused_computation.13 | convolution fusion | flops 135528448 | bytes 5373956 | tf_op jit(solution)/shard_map/while/body/eval_jaxpr/cond/branch_1_fun/dot_general | solution.py:32
  91.6 1.9 %subtract_convert_fusion.25 = (bf16[256,256]{1,0:T(8,128)(2,1)}, bf16[256,256]{1,0:T(8,128)(2,1)}, bf16[256,256]{1,0:T(8,128)(2,1)S(1)}, bf16[256,256]{1,0:T(8,128)(2,1)}) fusion(s32[256]{0:T(256)S(1)} %get-tuple-element.688), kind=kLoop, calls=%fused_computation.62.clone.1 | loop fusion | flops 1441792 | bytes 525312 | tf_op jit(solution)/shard_map/convert_element_type | solution.py:9
  93.5 1.2 fusion.214
  94.7 1.2 subtract_convert_fusion.24
  95.9 13.5 %conditional.5 = ((f32[256,1024]{0,1:T(8,128)}, f32[256,1024]{0,1:T(8,128)}, f32[640,1024]{0,1:T(8,128)})) conditional(s32[]{:T(128)} %convert_element_type.670, (f32[256,1024]{0,1:T(8,128)}, f32[256,1024]{0,1:T(8,128)}, f32[640,1024]{0,1:T(8,128)}) %tuple.73, (s32[]{:T(128)}, bf16[4,128,1024]{2,1,0:T(8,128)(2,1)}, bf16[256,128]{1,0:T(8,128)(2,1)}, ...), branch_computations={%region_1.1_spmd, %region_2.2_spmd} | conditional | flops 1083179008 | bytes 39321852 | solution.py:111
  95.9 1.3 fusion.29
  97.1 1.3 fusion.22
  98.4 1.3 fusion.32
  99.7 5.0 %multiply_subtract_fusion = (f32[256,1024]{0,1:T(8,128)S(1)}, f32[256,1024]{0,1:T(8,128)S(1)}, f32[256,1024]{0,1:T(8,128)}, f32[256,1024]{0,1:T(8,128)}) fusion(f32[256,1024]{0,1:T(8,128)} %get-tuple-element.336, f32[256,1024]{0,1:T(8,128)S(1)} %fusion.22, f32[256,1024]{0,1:T(8,128)} %get-tuple-element.335, f32[256,1024]{0,1:T(8,128)} %get-tuple-element.323, ...), kind=kOutput, calls=%fused_computation.31 | convolution fusion | flops 71041024 | bytes 12910600 | tf_op jit(solution)/shard_map/while/body/eval_jaxpr/cond/branch_1_fun/dot_general | solution.py:22
  106.6 2.7 %fusion.20 = f32[640,1024]{0,1:T(8,128)} fusion(f32[640,1024]{0,1:T(8,128)} %get-tuple-element.334, s32[]{:T(128)S(6)} %select_n.24, f32[1024,256]{1,0:T(8,128)S(1)} %convolution_add_fusion.2, f32[1024,256]{1,0:T(8,128)S(1)} %convolution_add_fusion.1, bf16[256,256]{1,0:T(8,128)(2,1)S(1)} %copy-done.2, f32[256,1024]{0,1:T(8,128)S(1)} %get-tuple-element.545), kind=kOutput, calls=%fused_computation.13 | convolution fusion | flops 135528448 | bytes 5373956 | tf_op jit(solution)/shard_map/while/body/eval_jaxpr/cond/branch_1_fun/dot_general | solution.py:32
  109.3 1.9 %subtract_convert_fusion.25 = (bf16[256,256]{1,0:T(8,128)(2,1)}, bf16[256,256]{1,0:T(8,128)(2,1)}, bf16[256,256]{1,0:T(8,128)(2,1)S(1)}, bf16[256,256]{1,0:T(8,128)(2,1)}) fusion(s32[256]{0:T(256)S(1)} %get-tuple-element.688), kind=kLoop, calls=%fused_computation.62.clone.1 | loop fusion | flops 1441792 | bytes 525312 | tf_op jit(solution)/shard_map/convert_element_type | solution.py:9
  111.2 1.2 fusion.214
  112.4 1.2 subtract_convert_fusion.24
  113.6 13.4 %conditional.5 = ((f32[256,1024]{0,1:T(8,128)}, f32[256,1024]{0,1:T(8,128)}, f32[640,1024]{0,1:T(8,128)})) conditional(s32[]{:T(128)} %convert_element_type.670, (f32[256,1024]{0,1:T(8,128)}, f32[256,1024]{0,1:T(8,128)}, f32[640,1024]{0,1:T(8,128)}) %tuple.73, (s32[]{:T(128)}, bf16[4,128,1024]{2,1,0:T(8,128)(2,1)}, bf16[256,128]{1,0:T(8,128)(2,1)}, ...), branch_computations={%region_1.1_spmd, %region_2.2_spmd} | conditional | flops 1083179008 | bytes 39321852 | solution.py:111
  113.6 1.3 fusion.29
  114.9 1.3 fusion.22
  116.1 1.3 fusion.32
  117.4 5.0 %multiply_subtract_fusion = (f32[256,1024]{0,1:T(8,128)S(1)}, f32[256,1024]{0,1:T(8,128)S(1)}, f32[256,1024]{0,1:T(8,128)}, f32[256,1024]{0,1:T(8,128)}) fusion(f32[256,1024]{0,1:T(8,128)} %get-tuple-element.336, f32[256,1024]{0,1:T(8,128)S(1)} %fusion.22, f32[256,1024]{0,1:T(8,128)} %get-tuple-element.335, f32[256,1024]{0,1:T(8,128)} %get-tuple-element.323, ...), kind=kOutput, calls=%fused_computation.31 | convolution fusion | flops 71041024 | bytes 12910600 | tf_op jit(solution)/shard_map/while/body/eval_jaxpr/cond/branch_1_fun/dot_general | solution.py:22
  124.4 2.6 %fusion.20 = f32[640,1024]{0,1:T(8,128)} fusion(f32[640,1024]{0,1:T(8,128)} %get-tuple-element.334, s32[]{:T(128)S(6)} %select_n.24, f32[1024,256]{1,0:T(8,128)S(1)} %convolution_add_fusion.2, f32[1024,256]{1,0:T(8,128)S(1)} %convolution_add_fusion.1, bf16[256,256]{1,0:T(8,128)(2,1)S(1)} %copy-done.2, f32[256,1024]{0,1:T(8,128)S(1)} %get-tuple-element.545), kind=kOutput, calls=%fused_computation.13 | convolution fusion | flops 135528448 | bytes 5373956 | tf_op jit(solution)/shard_map/while/body/eval_jaxpr/cond/branch_1_fun/dot_general | solution.py:32
  127.0 1.9 %subtract_convert_fusion.25 = (bf16[256,256]{1,0:T(8,128)(2,1)}, bf16[256,256]{1,0:T(8,128)(2,1)}, bf16[256,256]{1,0:T(8,128)(2,1)S(1)}, bf16[256,256]{1,0:T(8,128)(2,1)}) fusion(s32[256]{0:T(256)S(1)} %get-tuple-element.688), kind=kLoop, calls=%fused_computation.62.clone.1 | loop fusion | flops 1441792 | bytes 525312 | tf_op jit(solution)/shard_map/convert_element_type | solution.py:9
  128.9 1.2 fusion.214
  130.1 1.2 subtract_convert_fusion.24
  131.2 13.4 %conditional.5 = ((f32[256,1024]{0,1:T(8,128)}, f32[256,1024]{0,1:T(8,128)}, f32[640,1024]{0,1:T(8,128)})) conditional(s32[]{:T(128)} %convert_element_type.670, (f32[256,1024]{0,1:T(8,128)}, f32[256,1024]{0,1:T(8,128)}, f32[640,1024]{0,1:T(8,128)}) %tuple.73, (s32[]{:T(128)}, bf16[4,128,1024]{2,1,0:T(8,128)(2,1)}, bf16[256,128]{1,0:T(8,128)(2,1)}, ...), branch_computations={%region_1.1_spmd, %region_2.2_spmd} | conditional | flops 1083179008 | bytes 39321852 | solution.py:111
  131.2 1.3 fusion.29
  132.5 1.3 fusion.22
  133.8 1.3 fusion.32
  135.1 5.0 %multiply_subtract_fusion = (f32[256,1024]{0,1:T(8,128)S(1)}, f32[256,1024]{0,1:T(8,128)S(1)}, f32[256,1024]{0,1:T(8,128)}, f32[256,1024]{0,1:T(8,128)}) fusion(f32[256,1024]{0,1:T(8,128)} %get-tuple-element.336, f32[256,1024]{0,1:T(8,128)S(1)} %fusion.22, f32[256,1024]{0,1:T(8,128)} %get-tuple-element.335, f32[256,1024]{0,1:T(8,128)} %get-tuple-element.323, ...), kind=kOutput, calls=%fused_computation.31 | convolution fusion | flops 71041024 | bytes 12910600 | tf_op jit(solution)/shard_map/while/body/eval_jaxpr/cond/branch_1_fun/dot_general | solution.py:22
  142.0 2.6 %fusion.20 = f32[640,1024]{0,1:T(8,128)} fusion(f32[640,1024]{0,1:T(8,128)} %get-tuple-element.334, s32[]{:T(128)S(6)} %select_n.24, f32[1024,256]{1,0:T(8,128)S(1)} %convolution_add_fusion.2, f32[1024,256]{1,0:T(8,128)S(1)} %convolution_add_fusion.1, bf16[256,256]{1,0:T(8,128)(2,1)S(1)} %copy-done.2, f32[256,1024]{0,1:T(8,128)S(1)} %get-tuple-element.545), kind=kOutput, calls=%fused_computation.13 | convolution fusion | flops 135528448 | bytes 5373956 | tf_op jit(solution)/shard_map/while/body/eval_jaxpr/cond/branch_1_fun/dot_general | solution.py:32
  144.7 2.0 %copy.14 = bf16[640,1024]{1,0:T(8,128)(2,1)S(1)} copy(f32[640,1024]{0,1:T(8,128)} %get-tuple-element.374) | data formatting | bytes 3932160 | tf_op jit(solution)/shard_map/while | solution.py:113
  146.6 1.1 slice.12
  147.7 2.0 %fusion.131 = f32[128,1024]{1,0:T(8,128)S(1)} fusion(s32[128]{0:T(128)S(1)} %iota_add_fusion.1, f32[256,1024]{0,1:T(8,128)} %get-tuple-element.373), kind=kOutput, calls=%fused_computation.158 | convolution fusion | flops 67862528 | bytes 1573376 | tf_op jit(solution)/shard_map/dot_general | solution.py:30
  149.7 2.0 %fusion.135 = f32[128,1024]{1,0:T(8,128)S(1)} fusion(s32[128]{0:T(128)S(1)} %iota_add_fusion.1, f32[256,1024]{0,1:T(8,128)} %get-tuple-element.372), kind=kOutput, calls=%fused_computation.159 | convolution fusion | flops 67862528 | bytes 1573376 | tf_op jit(solution)/shard_map/dot_general | solution.py:30
  151.7 2.3 %convolution_add_fusion.9 = f32[128,1024]{1,0:T(8,128)S(1)} fusion(f32[128,1024]{1,0:T(8,128)S(1)} %fusion.131, f32[256,1024]{0,1:T(8,128)} %get-tuple-element.373, s32[128]{0:T(128)S(1)} %iota_add_fusion.1), kind=kOutput, calls=%fused_computation.98 | convolution fusion | flops 68780032 | bytes 2097664 | tf_op jit(solution)/shard_map/dot_general | solution.py:31
  154.0 2.3 %convolution_add_fusion.11 = f32[128,1024]{1,0:T(8,128)S(1)} fusion(f32[128,1024]{1,0:T(8,128)S(1)} %fusion.135, f32[256,1024]{0,1:T(8,128)} %get-tuple-element.372, s32[128]{0:T(128)S(1)} %iota_add_fusion.1), kind=kOutput, calls=%fused_computation.100 | convolution fusion | flops 68780032 | bytes 2097664 | tf_op jit(solution)/shard_map/dot_general | solution.py:31
  156.3 2.0 %convolution_add_fusion.10 = f32[128,1024]{1,0:T(8,128)S(1)} fusion(f32[128,1024]{1,0:T(8,128)S(1)} %convolution_add_fusion.11, s32[128]{0:T(128)S(1)} %iota_add_fusion.1, f32[256,1024]{0,1:T(8,128)} %get-tuple-element.372), kind=kOutput, calls=%fused_computation.99 | convolution fusion | flops 68091904 | bytes 2097664 | tf_op jit(solution)/shard_map/dot_general | solution.py:32
  158.3 2.7 %fusion.74 = bf16[128,1024]{1,0:T(8,128)(2,1)} fusion(f32[128,1024]{1,0:T(8,128)S(1)} %convolution_add_fusion.10, f32[128,1024]{1,0:T(8,128)S(1)} %convolution_add_fusion.9, bf16[128,1024]{1,0:T(8,128)(2,1)S(1)} %copy-done.5, f32[1024]{0:T(1024)S(1)} %copy-done.6, s32[128]{0:T(128)S(1)} %iota_add_fusion.1, f32[256,1024]{0,1:T(8,128)} %get-tuple-element.373), kind=kOutput, calls=%fused_computation.101 | convolution fusion | flops 68878336 | bytes 2626048 | tf_op jit(solution)/shard_map/dot_general | solution.py:32
  161.0 12.1 %reduce-scatter.2.cloned.1.call-done = bf16[128,1024]{1,0:T(8,128)(2,1)} async-done(((bf16[512,1024]{1,0:T(8,128)(2,1)}), bf16[128,1024]{1,0:T(8,128)(2,1)}) %reduce-scatter.2.cloned.1.call-update) | async-done | bytes 262160 | tf_op jit(solution)/shard_map/reduce_scatter | solution.py:118
  173.2 1.8 convert_element_type.265
  (62 shorter events, 9.8 us)
Async XLA Ops:
  7.2 2.7 %copy-start = (bf16[128,1024]{1,0:T(8,128)(2,1)S(1)}, bf16[128,1024]{1,0:T(8,128)(2,1)}, u32[]{:S(2)}) copy-start(bf16[128,1024]{1,0:T(8,128)(2,1)} %param.11) | copy-start | bytes 786436
  7.2 33.1 %all-gather.4.cloned.1.call-start = ((), (), s32[]{:S(2)}) async-start(), calls=%async_computation.1 | async-start | bytes 1310720 | tf_op jit(solution)/shard_map/all_gather | solution.py:72
  7.9 62.1 %all-gather.6.cloned.1.call-start = ((), (), s32[]{:S(2)}) async-start(), calls=%async_computation.3 | async-start | bytes 1310720 | tf_op jit(solution)/shard_map/all_gather | solution.py:99
  9.8 163.4 %reduce-scatter.2.cloned.1.call-start = ((), (), s32[]{:S(2)}) async-start(), calls=%async_computation.2 | async-start | bytes 1310720 | tf_op jit(solution)/shard_map/reduce_scatter | solution.py:118
  40.2 2.2 %copy-start.4 = (bf16[512,1024]{1,0:T(8,128)(2,1)S(1)}, bf16[512,1024]{1,0:T(8,128)(2,1)}, u32[]{:S(2)}) copy-start(bf16[512,1024]{1,0:T(8,128)(2,1)} %all-gather.4.cloned.1.call-done) | copy-start | bytes 3145732
  87.0 0.9 copy-start.1
  87.3 1.3 copy-start.3
  87.9 1.0 copy-start.2
  104.7 0.9 copy-start.1
  105.0 1.2 copy-start.3
  105.6 1.0 copy-start.2
  122.4 0.9 copy-start.1
  122.8 1.2 copy-start.3
  123.3 1.0 copy-start.2
  140.1 0.9 copy-start.1
  140.4 1.3 copy-start.3
  141.0 1.0 copy-start.2
  149.7 8.6 %copy-start.5 = (bf16[128,1024]{1,0:T(8,128)(2,1)S(1)}, bf16[128,1024]{1,0:T(8,128)(2,1)}, u32[]{:S(2)}) copy-start(bf16[128,1024]{1,0:T(8,128)(2,1)} %multiply_convert_fusion) | copy-start | bytes 786436
  149.7 8.6 %copy-start.6 = (f32[1024]{0:T(1024)S(1)}, f32[1024]{0:T(1024)}, u32[]{:S(2)}) copy-start(f32[1024]{0:T(1024)} %param.13) | copy-start | bytes 12292
Sparse Core Ops, SparseCore 0:
  9.6 30.6 all-gather.3
  42.4 27.5 all-gather.5
  147.8 25.2 reduce-scatter.1
where the time goes:
time: 182 us; the launch traced here: 181 us
  matrix products  79.1 us (43%)
  waiting for transfers between devices  54 us (30%)
  other arithmetic  20.7 us (11%)
  between operations  13.9 us (8%)
  local copies, waits for them, and re-layouts  13.3 us (7%)
    dot_general x10, matrix products, table_times(): jnp.dot(low_part, signal, preferred_element_type=jnp.float32)  26.5 us
    all_gather x1, waiting for transfers between devices, shards(): taps = lax.all_gather(filter_taps, 'ctx', axis=0, tiled=True)  24.8 us
    dot_general x10, matrix products, table_times_float(): jnp.dot(low_part, value_high, preferred_element_type=jnp.float32)  16.6 us
    all_gather x1, waiting for transfers between devices, shards(): spans = lax.all_gather(grad_y[None], 'ctx', axis=0, tiled=True)  16.3 us
    convert_element_type x8, other arithmetic, split_parts(): low_part = (values - high_part.astype(jnp.float32)).astype(jnp.bfloat16)  12.4 us
    reduce_scatter x1, waiting for transfers between devices, shards(): lax.psum_scatter(lag_sums[span_len:].astype(jnp.bfloat16), 'ctx', scatter...  12.1 us
    dot_general x10, matrix products, table_times(): jnp.dot(high_part, signal, preferred_element_type=jnp.float32)  11.6 us
    dot_general x10, matrix products, table_times_float(): jnp.dot(high_part, value_low, preferred_element_type=jnp.float32)  7.3 us
  transfers between devices with their start and end apart: 3, of which 3 were waited for; matrix products, arithmetic and copies ran while one was open for 19% of the time, Pallas kernels for 0%

commit v1 on v0

--- a/solution.py
+++ b/solution.py
@@ -2,6 +2,22 @@
 import jax.numpy as jnp
 from jax import lax
 from jax.sharding import PartitionSpec as P
+
+
+def collect(x, axis, dim):
+    ways, here, step = (lax.axis_size(axis), lax.axis_index(axis), x.shape[dim])
+    shape = [n * ways if d == dim else n for d, n in enumerate(x.shape)]
+    full = lax.dynamic_update_slice_in_dim(jnp.zeros(shape, x.dtype), x, here * step, axis=dim)
+    going_up = going_down = x
+    for far in range(1, ways // 2 + 1):
+        going_up = lax.ppermute(going_up, axis, [(d, (d + 1) % ways) for d in range(ways)])
+        full = lax.dynamic_update_slice_in_dim(full, going_up, (here - far) % ways * step, axis=dim)
+        if 2 * far < ways:
+            going_down = lax.ppermute(going_down, axis, [(d, (d - 1) % ways) for d in range(ways)])
+            full = lax.dynamic_update_slice_in_dim(
+                full, going_down, (here + far) % ways * step, axis=dim
+            )
+    return full
 
 
 def split_parts(values):
@@ -69,7 +85,7 @@
     full_fwd = phase_tables(period, period, 0, period)
     short_inv = phase_tables(span_len, period, span_len, period)
     full_inv = phase_tables(period, period, span_len, period)
-    taps = lax.all_gather(filter_taps, "ctx", axis=0, tiled=True)
+    taps = collect(filter_taps, "ctx", 0)
     taps_padded = jnp.concatenate([jnp.zeros((span_len, channels), jnp.bfloat16), taps], axis=0)
     windows = jnp.concatenate(
         [

time: 182 us -> 162 us (0.89)
  waiting for transfers between devices: 54 us -> 23.4 us
  starting transfers between devices: 0.12 us -> 5.31 us
  local copies, waits for them, and re-layouts: 13.3 us -> 16.2 us
  matrix products: 79.1 us -> 81 us
    all_gather x1 -> x0, waiting for transfers between devices: 24.8 us -> none  [shards(): taps = lax.all_gather(filter_taps, 'ctx', axis=0, tiled=True)]
    all_gather x1, waiting for transfers between devices: 16.3 us -> 0.01 us  [shards(): spans = lax.all_gather(grad_y[None], 'ctx', axis=0, tiled=True)]
    ppermute x0 -> x3, waiting for transfers between devices: none -> 11.2 us  [the longest x2 11.2 us: collect(): lax.ppermute(going_up, axis, [(d, (d + 1) % ways) for d in range(ways)])]
    ppermute x0 -> x3, starting transfers between devices: none -> 5.23 us  [the longest x2 3.14 us: collect(): lax.ppermute(going_up, axis, [(d, (d + 1) % ways) for d in range(ways)])]
    dynamic_update_slice x0 -> x4, local copies, waits for them, and re-layouts: none -> 3.96 us  [the longest x2 1.94 us: collect(): lax.dynamic_update_slice_in_dim(full, going_up, (here - far) % ways * ste...]
    dot_general x10, matrix products: 26.5 us -> 28.5 us  [table_times(): jnp.dot(low_part, signal, preferred_element_type=jnp.float32)]
  transfers between devices with their start and end apart: 3 -> 5, of which waited for: 3 -> 2; matrix products, arithmetic and copies ran while one was open for 19% -> 24% of each run, Pallas kernels for 0% -> 0%
where the time goes in v1:
time: 162 us; the launch traced here: 161 us
  matrix products  81 us (50%)
  waiting for transfers between devices  23.4 us (14%)
  other arithmetic  20.7 us (13%)
  local copies, waits for them, and re-layouts  16.2 us (10%)
  between operations  14.3 us (9%)
  starting transfers between devices  5.31 us (3%)
    dot_general x10, matrix products, table_times(): jnp.dot(low_part, signal, preferred_element_type=jnp.float32)  28.5 us
    dot_general x10, matrix products, table_times_float(): jnp.dot(low_part, value_high, preferred_element_type=jnp.float32)  16.5 us
    convert_element_type x8, other arithmetic, split_parts(): low_part = (values - high_part.astype(jnp.float32)).astype(jnp.bfloat16)  12.4 us
    reduce_scatter x1, waiting for transfers between devices, shards(): lax.psum_scatter(lag_sums[span_len:].astype(jnp.bfloat16), 'ctx', scatter...  12.3 us
    dot_general x10, matrix products, table_times(): jnp.dot(high_part, signal, preferred_element_type=jnp.float32)  11.6 us
    ppermute x2, waiting for transfers between devices, collect(): lax.ppermute(going_up, axis, [(d, (d + 1) % ways) for d in range(ways)])  11.2 us
    dot_general x10, matrix products, table_times_float(): jnp.dot(high_part, value_low, preferred_element_type=jnp.float32)  7.3 us
    dot_general x2, matrix products, batched_times(): jnp.einsum('pr,nrc->npc', low_part, blocks, preferred_element_type=jnp.fl...  7.28 us
  transfers between devices with their start and end apart: 5, of which 2 were waited for; matrix products, arithmetic and copies ran while one was open for 24% of the time, Pallas kernels for 0%

profile of v1, /device:TPU:0, one launch (start us, length us, event | category | flops | bytes accessed | tf_op | source)
XLA Modules:
  0.0 161.4 jit_solution(13340014230642030902)
XLA Ops:
  7.2 3.1 %collective-permute-start = (bf16[128,1024]{1,0:T(8,128)(2,1)}, bf16[128,1024]{1,0:T(8,128)(2,1)}, u32[]{:S(2)}, u32[]{:S(2)}) collective-permute-start(bf16[128,1024]{1,0:T(8,128)(2,1)} %param.12), channel_id=1, source_target_pairs={{0,4},{4,8},{8,12},{12,0},{1,5},{5,9},{9,13},{13,1},{2,6},{6,10},{... | collective-permute-start | bytes 786440 | tf_op jit(solution)/shard_map/ppermute | solution.py:13
  10.3 2.1 %collective-permute-start.1 = (bf16[128,1024]{1,0:T(8,128)(2,1)}, bf16[128,1024]{1,0:T(8,128)(2,1)}, u32[]{:S(2)}, u32[]{:S(2)}) collective-permute-start(bf16[128,1024]{1,0:T(8,128)(2,1)} %param.12), channel_id=1, source_target_pairs={{0,12},{4,0},{8,4},{12,8},{1,13},{5,1},{9,5},{13,9},{2,14},{6,2},{... | collective-permute-start | bytes 786440 | tf_op jit(solution)/shard_map/ppermute | solution.py:16
  12.4 1.8 %multiply_convert_fusion = bf16[128,1024]{1,0:T(8,128)(2,1)} fusion(bf16[128,1024]{1,0:T(8,128)(2,1)} %param.10, bf16[128,1024]{1,0:T(8,128)(2,1)} %param.9), kind=kLoop, calls=%fused_computation.104 | loop fusion | flops 524288 | bytes 786432 | tf_op jit(solution)/shard_map/convert_element_type | solution.py:83
  15.7 1.7 %convolution_add_fusion.7 = f32[256,1024]{1,0:T(8,128)} fusion(f32[256,1024]{1,0:T(8,128)S(1)} %fusion.120, bf16[128,1024]{1,0:T(8,128)(2,1)S(1)} %copy-done), kind=kOutput, calls=%fused_computation.92 | convolution fusion | flops 67960832 | bytes 2359296 | tf_op jit(solution)/shard_map/dot_general | solution.py:38
  17.4 1.7 %fusion.70 = f32[256,1024]{1,0:T(8,128)} fusion(f32[256,1024]{1,0:T(8,128)S(1)} %fusion.117, bf16[128,1024]{1,0:T(8,128)(2,1)S(1)} %copy-done), kind=kOutput, calls=%fused_computation.91 | convolution fusion | flops 68222976 | bytes 2359296 | tf_op jit(solution)/shard_map/dot_general | solution.py:38
  19.3 1.0 constant_dynamic-update-slice_fusion.3
  20.5 1.4 copy.12
  21.8 1.3 copy.13
  24.1 1.0 constant_dynamic-update-slice_fusion.1
  25.1 11.1 %collective-permute-done.2 = bf16[128,1024]{1,0:T(8,128)(2,1)} collective-permute-done((bf16[128,1024]{1,0:T(8,128)(2,1)}, bf16[128,1024]{1,0:T(8,128)(2,1)}, u32[]{:S(2)}, u32[]{:S(2)}) %collective-permute-start.2) | collective-permute-done | bytes 262176 | tf_op jit(solution)/shard_map/ppermute | solution.py:13
  38.9 1.7 %fusion.91 = f32[4,1024,256]{2,1,0:T(8,128)S(1)} fusion(bf16[4,128,1024]{1,2,0:T(8,128)(2,1)S(1)} %copy.11, bf16[4,128,1024]{1,2,0:T(8,128)(2,1)S(1)} %copy.10), kind=kOutput, calls=%fused_computation.130 | convolution fusion | flops 542048256 | bytes 6291456 | tf_op jit(solution)/shard_map/pr,nrc->npc/dot_general | solution.py:65
  40.5 1.6 %fusion.93 = f32[4,1024,256]{2,1,0:T(8,128)S(1)} fusion(bf16[4,128,1024]{1,2,0:T(8,128)(2,1)S(1)} %copy.11, bf16[4,128,1024]{1,2,0:T(8,128)(2,1)S(1)} %copy.10), kind=kOutput, calls=%fused_computation.132 | convolution fusion | flops 542048256 | bytes 6291456 | tf_op jit(solution)/shard_map/pr,nrc->npc/dot_general | solution.py:65
  42.2 3.7 %negate_bitcast_fusion = f32[4,256,1024]{1,2,0:T(8,128)} fusion(f32[4,1024,256]{2,1,0:T(8,128)S(1)} %fusion.91, bf16[4,128,1024]{1,2,0:T(8,128)(2,1)S(1)} %copy.11, bf16[4,128,1024]{1,2,0:T(8,128)(2,1)S(1)} %copy.10), kind=kOutput, calls=%fused_computation.86 | convolution fusion | flops 544342016 | bytes 10485760 | tf_op jit(solution)/shard_map/pr,nrc->npc/dot_general | solution.py:67
  45.9 3.6 %add_bitcast_fusion = f32[4,256,1024]{1,2,0:T(8,128)} fusion(f32[4,1024,256]{2,1,0:T(8,128)S(1)} %fusion.93, bf16[4,128,1024]{1,2,0:T(8,128)(2,1)S(1)} %copy.11, bf16[4,128,1024]{1,2,0:T(8,128)(2,1)S(1)} %copy.10), kind=kOutput, calls=%fused_computation.87 | convolution fusion | flops 543293440 | bytes 10485760 | tf_op jit(solution)/shard_map/pr,nrc->npc/dot_general | solution.py:67
  49.5 1.7 %broadcast_in_dim.9 = f32[640,1024]{0,1:T(8,128)} broadcast(f32[]{:T(128)} %constant.113.clone.1), dimensions={} | broadcast | bytes 2621444 | tf_op jit(solution)/shard_map/broadcast_in_dim | solution.py:101
  51.2 1.0 broadcast_in_dim.8
  52.3 1.1 broadcast_in_dim.8.clone
  53.3 70.8 %while.20 = (s32[]{:T(128)}, f32[256,1024]{0,1:T(8,128)}, f32[256,1024]{0,1:T(8,128)}, f32[640,1024]{0,1:T(8,128)}, s32[]{:T(128)}, /*index=5*/bf16[4,128,1024]{...) while((s32[]{:T(128)}, f32[256,1024]{0,1:T(8,128)}, ...), condition=%wide.region_3.4_spmd.clone.clone.clone, body=%wide.region_0.3_spmd.clone.clone.clone.sunk | while | flops 1085865984 | bytes 40109640 | solution.py:129
  53.3 1.9 %subtract_convert_fusion.25 = (bf16[256,256]{1,0:T(8,128)(2,1)}, bf16[256,256]{1,0:T(8,128)(2,1)}, bf16[256,256]{1,0:T(8,128)(2,1)S(1)}, bf16[256,256]{1,0:T(8,128)(2,1)}) fusion(s32[256]{0:T(256)S(1)} %get-tuple-element.688), kind=kLoop, calls=%fused_computation.62.clone.1 | loop fusion | flops 1441792 | bytes 525312 | tf_op jit(solution)/shard_map/convert_element_type | solution.py:25
  55.2 1.2 fusion.214
  56.4 1.2 subtract_convert_fusion.24
  57.6 13.4 %conditional.5 = ((f32[256,1024]{0,1:T(8,128)}, f32[256,1024]{0,1:T(8,128)}, f32[640,1024]{0,1:T(8,128)})) conditional(s32[]{:T(128)} %convert_element_type.670, (f32[256,1024]{0,1:T(8,128)}, f32[256,1024]{0,1:T(8,128)}, f32[640,1024]{0,1:T(8,128)}) %tuple.73, (s32[]{:T(128)}, bf16[4,128,1024]{2,1,0:T(8,128)(2,1)}, bf16[256,128]{1,0:T(8,128)(2,1)}, ...), branch_computations={%region_1.1_spmd, %region_2.2_spmd} | conditional | flops 1083179008 | bytes 39321852 | solution.py:127
  57.6 1.3 fusion.29
  58.9 1.3 fusion.22
  60.1 1.3 fusion.32
  61.4 5.0 %multiply_subtract_fusion = (f32[256,1024]{0,1:T(8,128)S(1)}, f32[256,1024]{0,1:T(8,128)S(1)}, f32[256,1024]{0,1:T(8,128)}, f32[256,1024]{0,1:T(8,128)}) fusion(f32[256,1024]{0,1:T(8,128)} %get-tuple-element.336, f32[256,1024]{0,1:T(8,128)S(1)} %fusion.22, f32[256,1024]{0,1:T(8,128)} %get-tuple-element.335, f32[256,1024]{0,1:T(8,128)} %get-tuple-element.323, ...), kind=kOutput, calls=%fused_computation.31 | convolution fusion | flops 71041024 | bytes 12910600 | tf_op jit(solution)/shard_map/while/body/eval_jaxpr/cond/branch_1_fun/dot_general | solution.py:38
  68.4 2.6 %fusion.20 = f32[640,1024]{0,1:T(8,128)} fusion(f32[640,1024]{0,1:T(8,128)} %get-tuple-element.334, s32[]{:T(128)S(6)} %select_n.70, f32[1024,256]{1,0:T(8,128)S(1)} %convolution_add_fusion.2, f32[1024,256]{1,0:T(8,128)S(1)} %convolution_add_fusion.1, bf16[256,256]{1,0:T(8,128)(2,1)S(1)} %copy-done.2, f32[256,1024]{0,1:T(8,128)S(1)} %get-tuple-element.545), kind=kOutput, calls=%fused_computation.13 | convolution fusion | flops 135528448 | bytes 5373956 | tf_op jit(solution)/shard_map/while/body/eval_jaxpr/cond/branch_1_fun/dot_general | solution.py:48
  71.0 1.9 %subtract_convert_fusion.25 = (bf16[256,256]{1,0:T(8,128)(2,1)}, bf16[256,256]{1,0:T(8,128)(2,1)}, bf16[256,256]{1,0:T(8,128)(2,1)S(1)}, bf16[256,256]{1,0:T(8,128)(2,1)}) fusion(s32[256]{0:T(256)S(1)} %get-tuple-element.688), kind=kLoop, calls=%fused_computation.62.clone.1 | loop fusion | flops 1441792 | bytes 525312 | tf_op jit(solution)/shard_map/convert_element_type | solution.py:25
  72.9 1.2 fusion.214
  74.1 1.2 subtract_convert_fusion.24
  75.3 13.4 %conditional.5 = ((f32[256,1024]{0,1:T(8,128)}, f32[256,1024]{0,1:T(8,128)}, f32[640,1024]{0,1:T(8,128)})) conditional(s32[]{:T(128)} %convert_element_type.670, (f32[256,1024]{0,1:T(8,128)}, f32[256,1024]{0,1:T(8,128)}, f32[640,1024]{0,1:T(8,128)}) %tuple.73, (s32[]{:T(128)}, bf16[4,128,1024]{2,1,0:T(8,128)(2,1)}, bf16[256,128]{1,0:T(8,128)(2,1)}, ...), branch_computations={%region_1.1_spmd, %region_2.2_spmd} | conditional | flops 1083179008 | bytes 39321852 | solution.py:127
  75.3 1.3 fusion.29
  76.5 1.3 fusion.22
  77.8 1.3 fusion.32
  79.1 5.0 %multiply_subtract_fusion = (f32[256,1024]{0,1:T(8,128)S(1)}, f32[256,1024]{0,1:T(8,128)S(1)}, f32[256,1024]{0,1:T(8,128)}, f32[256,1024]{0,1:T(8,128)}) fusion(f32[256,1024]{0,1:T(8,128)} %get-tuple-element.336, f32[256,1024]{0,1:T(8,128)S(1)} %fusion.22, f32[256,1024]{0,1:T(8,128)} %get-tuple-element.335, f32[256,1024]{0,1:T(8,128)} %get-tuple-element.323, ...), kind=kOutput, calls=%fused_computation.31 | convolution fusion | flops 71041024 | bytes 12910600 | tf_op jit(solution)/shard_map/while/body/eval_jaxpr/cond/branch_1_fun/dot_general | solution.py:38
  86.0 2.6 %fusion.20 = f32[640,1024]{0,1:T(8,128)} fusion(f32[640,1024]{0,1:T(8,128)} %get-tuple-element.334, s32[]{:T(128)S(6)} %select_n.70, f32[1024,256]{1,0:T(8,128)S(1)} %convolution_add_fusion.2, f32[1024,256]{1,0:T(8,128)S(1)} %convolution_add_fusion.1, bf16[256,256]{1,0:T(8,128)(2,1)S(1)} %copy-done.2, f32[256,1024]{0,1:T(8,128)S(1)} %get-tuple-element.545), kind=kOutput, calls=%fused_computation.13 | convolution fusion | flops 135528448 | bytes 5373956 | tf_op jit(solution)/shard_map/while/body/eval_jaxpr/cond/branch_1_fun/dot_general | solution.py:48
  88.7 1.9 %subtract_convert_fusion.25 = (bf16[256,256]{1,0:T(8,128)(2,1)}, bf16[256,256]{1,0:T(8,128)(2,1)}, bf16[256,256]{1,0:T(8,128)(2,1)S(1)}, bf16[256,256]{1,0:T(8,128)(2,1)}) fusion(s32[256]{0:T(256)S(1)} %get-tuple-element.688), kind=kLoop, calls=%fused_computation.62.clone.1 | loop fusion | flops 1441792 | bytes 525312 | tf_op jit(solution)/shard_map/convert_element_type | solution.py:25
  90.6 1.2 fusion.214
  91.8 1.2 subtract_convert_fusion.24
  93.0 13.4 %conditional.5 = ((f32[256,1024]{0,1:T(8,128)}, f32[256,1024]{0,1:T(8,128)}, f32[640,1024]{0,1:T(8,128)})) conditional(s32[]{:T(128)} %convert_element_type.670, (f32[256,1024]{0,1:T(8,128)}, f32[256,1024]{0,1:T(8,128)}, f32[640,1024]{0,1:T(8,128)}) %tuple.73, (s32[]{:T(128)}, bf16[4,128,1024]{2,1,0:T(8,128)(2,1)}, bf16[256,128]{1,0:T(8,128)(2,1)}, ...), branch_computations={%region_1.1_spmd, %region_2.2_spmd} | conditional | flops 1083179008 | bytes 39321852 | solution.py:127
  93.0 1.3 fusion.29
  94.3 1.3 fusion.22
  95.5 1.3 fusion.32
  96.8 5.0 %multiply_subtract_fusion = (f32[256,1024]{0,1:T(8,128)S(1)}, f32[256,1024]{0,1:T(8,128)S(1)}, f32[256,1024]{0,1:T(8,128)}, f32[256,1024]{0,1:T(8,128)}) fusion(f32[256,1024]{0,1:T(8,128)} %get-tuple-element.336, f32[256,1024]{0,1:T(8,128)S(1)} %fusion.22, f32[256,1024]{0,1:T(8,128)} %get-tuple-element.335, f32[256,1024]{0,1:T(8,128)} %get-tuple-element.323, ...), kind=kOutput, calls=%fused_computation.31 | convolution fusion | flops 71041024 | bytes 12910600 | tf_op jit(solution)/shard_map/while/body/eval_jaxpr/cond/branch_1_fun/dot_general | solution.py:38
  103.8 2.7 %fusion.20 = f32[640,1024]{0,1:T(8,128)} fusion(f32[640,1024]{0,1:T(8,128)} %get-tuple-element.334, s32[]{:T(128)S(6)} %select_n.70, f32[1024,256]{1,0:T(8,128)S(1)} %convolution_add_fusion.2, f32[1024,256]{1,0:T(8,128)S(1)} %convolution_add_fusion.1, bf16[256,256]{1,0:T(8,128)(2,1)S(1)} %copy-done.2, f32[256,1024]{0,1:T(8,128)S(1)} %get-tuple-element.545), kind=kOutput, calls=%fused_computation.13 | convolution fusion | flops 135528448 | bytes 5373956 | tf_op jit(solution)/shard_map/while/body/eval_jaxpr/cond/branch_1_fun/dot_general | solution.py:48
  106.4 1.9 %subtract_convert_fusion.25 = (bf16[256,256]{1,0:T(8,128)(2,1)}, bf16[256,256]{1,0:T(8,128)(2,1)}, bf16[256,256]{1,0:T(8,128)(2,1)S(1)}, bf16[256,256]{1,0:T(8,128)(2,1)}) fusion(s32[256]{0:T(256)S(1)} %get-tuple-element.688), kind=kLoop, calls=%fused_computation.62.clone.1 | loop fusion | flops 1441792 | bytes 525312 | tf_op jit(solution)/shard_map/convert_element_type | solution.py:25
  108.4 1.2 fusion.214
  109.5 1.2 subtract_convert_fusion.24
  110.7 13.4 %conditional.5 = ((f32[256,1024]{0,1:T(8,128)}, f32[256,1024]{0,1:T(8,128)}, f32[640,1024]{0,1:T(8,128)})) conditional(s32[]{:T(128)} %convert_element_type.670, (f32[256,1024]{0,1:T(8,128)}, f32[256,1024]{0,1:T(8,128)}, f32[640,1024]{0,1:T(8,128)}) %tuple.73, (s32[]{:T(128)}, bf16[4,128,1024]{2,1,0:T(8,128)(2,1)}, bf16[256,128]{1,0:T(8,128)(2,1)}, ...), branch_computations={%region_1.1_spmd, %region_2.2_spmd} | conditional | flops 1083179008 | bytes 39321852 | solution.py:127
  110.7 1.3 fusion.29
  112.0 1.3 fusion.22
  113.3 1.3 fusion.32
  114.6 5.0 %multiply_subtract_fusion = (f32[256,1024]{0,1:T(8,128)S(1)}, f32[256,1024]{0,1:T(8,128)S(1)}, f32[256,1024]{0,1:T(8,128)}, f32[256,1024]{0,1:T(8,128)}) fusion(f32[256,1024]{0,1:T(8,128)} %get-tuple-element.336, f32[256,1024]{0,1:T(8,128)S(1)} %fusion.22, f32[256,1024]{0,1:T(8,128)} %get-tuple-element.335, f32[256,1024]{0,1:T(8,128)} %get-tuple-element.323, ...), kind=kOutput, calls=%fused_computation.31 | convolution fusion | flops 71041024 | bytes 12910600 | tf_op jit(solution)/shard_map/while/body/eval_jaxpr/cond/branch_1_fun/dot_general | solution.py:38
  121.5 2.6 %fusion.20 = f32[640,1024]{0,1:T(8,128)} fusion(f32[640,1024]{0,1:T(8,128)} %get-tuple-element.334, s32[]{:T(128)S(6)} %select_n.70, f32[1024,256]{1,0:T(8,128)S(1)} %convolution_add_fusion.2, f32[1024,256]{1,0:T(8,128)S(1)} %convolution_add_fusion.1, bf16[256,256]{1,0:T(8,128)(2,1)S(1)} %copy-done.2, f32[256,1024]{0,1:T(8,128)S(1)} %get-tuple-element.545), kind=kOutput, calls=%fused_computation.13 | convolution fusion | flops 135528448 | bytes 5373956 | tf_op jit(solution)/shard_map/while/body/eval_jaxpr/cond/branch_1_fun/dot_general | solution.py:48
  124.1 2.0 %copy.14 = bf16[640,1024]{1,0:T(8,128)(2,1)S(1)} copy(f32[640,1024]{0,1:T(8,128)} %get-tuple-element.374) | data formatting | bytes 3932160 | tf_op jit(solution)/shard_map/while | solution.py:129
  126.0 1.1 slice.12
  127.2 2.0 %fusion.131 = f32[128,1024]{1,0:T(8,128)S(1)} fusion(s32[128]{0:T(128)S(1)} %iota_add_fusion.1, f32[256,1024]{0,1:T(8,128)} %get-tuple-element.373), kind=kOutput, calls=%fused_computation.158 | convolution fusion | flops 67862528 | bytes 1573376 | tf_op jit(solution)/shard_map/dot_general | solution.py:46
  129.1 2.0 %fusion.135 = f32[128,1024]{1,0:T(8,128)S(1)} fusion(s32[128]{0:T(128)S(1)} %iota_add_fusion.1, f32[256,1024]{0,1:T(8,128)} %get-tuple-element.372), kind=kOutput, calls=%fused_computation.159 | convolution fusion | flops 67862528 | bytes 1573376 | tf_op jit(solution)/shard_map/dot_general | solution.py:46
  131.1 2.3 %convolution_add_fusion.9 = f32[128,1024]{1,0:T(8,128)S(1)} fusion(f32[128,1024]{1,0:T(8,128)S(1)} %fusion.131, f32[256,1024]{0,1:T(8,128)} %get-tuple-element.373, s32[128]{0:T(128)S(1)} %iota_add_fusion.1), kind=kOutput, calls=%fused_computation.98 | convolution fusion | flops 68780032 | bytes 2097664 | tf_op jit(solution)/shard_map/dot_general | solution.py:47
  133.5 2.3 %convolution_add_fusion.11 = f32[128,1024]{1,0:T(8,128)S(1)} fusion(f32[128,1024]{1,0:T(8,128)S(1)} %fusion.135, f32[256,1024]{0,1:T(8,128)} %get-tuple-element.372, s32[128]{0:T(128)S(1)} %iota_add_fusion.1), kind=kOutput, calls=%fused_computation.100 | convolution fusion | flops 68780032 | bytes 2097664 | tf_op jit(solution)/shard_map/dot_general | solution.py:47
  135.8 2.0 %convolution_add_fusion.10 = f32[128,1024]{1,0:T(8,128)S(1)} fusion(f32[128,1024]{1,0:T(8,128)S(1)} %convolution_add_fusion.11, s32[128]{0:T(128)S(1)} %iota_add_fusion.1, f32[256,1024]{0,1:T(8,128)} %get-tuple-element.372), kind=kOutput, calls=%fused_computation.99 | convolution fusion | flops 68091904 | bytes 2097664 | tf_op jit(solution)/shard_map/dot_general | solution.py:48
  137.8 2.7 %fusion.74 = bf16[128,1024]{1,0:T(8,128)(2,1)} fusion(f32[128,1024]{1,0:T(8,128)S(1)} %convolution_add_fusion.10, f32[128,1024]{1,0:T(8,128)S(1)} %convolution_add_fusion.9, bf16[128,1024]{1,0:T(8,128)(2,1)S(1)} %copy-done.6, f32[1024]{0:T(1024)S(1)} %copy-done.7, s32[128]{0:T(128)S(1)} %iota_add_fusion.1, f32[256,1024]{0,1:T(8,128)} %get-tuple-element.373), kind=kOutput, calls=%fused_computation.101 | convolution fusion | flops 68878336 | bytes 2626048 | tf_op jit(solution)/shard_map/dot_general | solution.py:48
  140.5 12.3 %reduce-scatter.2.cloned.1.call-done = bf16[128,1024]{1,0:T(8,128)(2,1)} async-done(((bf16[512,1024]{1,0:T(8,128)(2,1)}), bf16[128,1024]{1,0:T(8,128)(2,1)}) %reduce-scatter.2.cloned.1.call-update) | async-done | bytes 262160 | tf_op jit(solution)/shard_map/reduce_scatter | solution.py:134
  152.7 1.8 %convert_element_type.265 = f32[128,1024]{1,0:T(8,128)} convert(bf16[128,1024]{1,0:T(8,128)(2,1)} %reduce-scatter.2.cloned.1.call-done) | non-fusion elementwise | flops 131072 | bytes 786432 | tf_op jit(solution)/shard_map/convert_element_type | solution.py:136
  (72 shorter events, 12.9 us)
Async XLA Ops:
  7.2 7.1 %copy-start = (bf16[128,1024]{1,0:T(8,128)(2,1)S(1)}, bf16[128,1024]{1,0:T(8,128)(2,1)}, u32[]{:S(2)}) copy-start(bf16[128,1024]{1,0:T(8,128)(2,1)} %param.11) | copy-start | bytes 786436
  7.2 42.3 %all-gather.3.cloned.1.call-start = ((), (), s32[]{:S(2)}) async-start(), calls=%async_computation.2 | async-start | bytes 1310720 | tf_op jit(solution)/shard_map/all_gather | solution.py:115
  7.2 13.1 %collective-permute-start = (bf16[128,1024]{1,0:T(8,128)(2,1)}, bf16[128,1024]{1,0:T(8,128)(2,1)}, u32[]{:S(2)}, u32[]{:S(2)}) collective-permute-start(bf16[128,1024]{1,0:T(8,128)(2,1)} %param.12), channel_id=1, source_target_pairs={{0,4},{4,8},{8,12},{12,0},{1,5},{5,9},{9,13},{13,1},{2,6},{6,10},{... | collective-permute-start | bytes 786440 | tf_op jit(solution)/shard_map/ppermute | solution.py:13
  10.3 13.8 %collective-permute-start.1 = (bf16[128,1024]{1,0:T(8,128)(2,1)}, bf16[128,1024]{1,0:T(8,128)(2,1)}, u32[]{:S(2)}, u32[]{:S(2)}) collective-permute-start(bf16[128,1024]{1,0:T(8,128)(2,1)} %param.12), channel_id=1, source_target_pairs={{0,12},{4,0},{8,4},{12,8},{1,13},{5,1},{9,5},{13,9},{2,14},{6,2},{... | collective-permute-start | bytes 786440 | tf_op jit(solution)/shard_map/ppermute | solution.py:16
  14.2 138.5 %reduce-scatter.2.cloned.1.call-start = ((), (), s32[]{:S(2)}) async-start(), calls=%async_computation.1 | async-start | bytes 1310720 | tf_op jit(solution)/shard_map/reduce_scatter | solution.py:134
  17.4 3.0 %copy-start.4 = (f32[256,1024]{1,0:T(8,128)S(1)}, f32[256,1024]{1,0:T(8,128)}, u32[]{:S(2)}) copy-start(f32[256,1024]{1,0:T(8,128)} %convolution_add_fusion.7) | copy-start | bytes 3145732
  19.1 2.7 %copy-start.5 = (f32[256,1024]{1,0:T(8,128)S(1)}, f32[256,1024]{1,0:T(8,128)}, u32[]{:S(2)}) copy-start(f32[256,1024]{1,0:T(8,128)} %fusion.70) | copy-start | bytes 3145732
  20.3 15.9 %collective-permute-start.2 = (bf16[128,1024]{1,0:T(8,128)(2,1)}, bf16[128,1024]{1,0:T(8,128)(2,1)}, u32[]{:S(2)}, u32[]{:S(2)}) collective-permute-start(bf16[128,1024]{1,0:T(8,128)(2,1)} %collective-permute-done), channel_id=1, source_target_pairs={{0,4},{4,8},{8,12},{12,0},{1,5},{5,9},{9,13},{13,1},{2,6},{6,10},{... | collective-permute-start | bytes 786440 | tf_op jit(solution)/shard_map/ppermute | solution.py:13
  66.4 0.9 copy-start.1
  66.8 1.3 copy-start.3
  67.3 1.0 copy-start.2
  84.1 0.9 copy-start.1
  84.4 1.2 copy-start.3
  85.0 1.0 copy-start.2
  101.8 0.9 copy-start.1
  102.2 1.2 copy-start.3
  102.7 1.0 copy-start.2
  119.5 0.9 copy-start.1
  119.9 1.2 copy-start.3
  120.5 1.0 copy-start.2
  129.1 8.6 %copy-start.6 = (bf16[128,1024]{1,0:T(8,128)(2,1)S(1)}, bf16[128,1024]{1,0:T(8,128)(2,1)}, u32[]{:S(2)}) copy-start(bf16[128,1024]{1,0:T(8,128)(2,1)} %multiply_convert_fusion) | copy-start | bytes 786436
  129.1 8.6 %copy-start.7 = (f32[1024]{0:T(1024)S(1)}, f32[1024]{0:T(1024)}, u32[]{:S(2)}) copy-start(f32[1024]{0:T(1024)} %param.13) | copy-start | bytes 12292
Sparse Core Ops, SparseCore 0:
  14.3 33.0 all-gather.2
  127.3 25.4 reduce-scatter.1
